TPU v7x, 1024 devices: a whole 8x8x8 slice. The times are simulated.
1024 devices in a mesh: tm: 32 (over y_hi, x, core), height: 4 (over y_lo), fsdp: 8 (over z).
Axes of the slice: x: 8, y: 8 (y_hi: 2, y_lo: 4; y = y_hi * 4 + y_lo), z: 8, core: 2. Of those that a mesh axis runs over, the one named last changes fastest.
Arguments:
- query_primal: bfloat16 [8, 128, 16, 8, 1536], P('fsdp', 'tm', 'height'), may hold values from -125 to 125
- key_primal: bfloat16 [8, 128, 16, 8, 1536], P('fsdp', 'tm', 'height'), may hold values from -5 to 5
- value_primal: bfloat16 [8, 128, 16, 8, 1536], P('fsdp', 'tm', 'height'), may hold values from -6 to 6
- query_tangent: bfloat16 [8, 128, 16, 8, 1536], P('fsdp', 'tm', 'height'), may hold values from -6 to 6
- key_tangent: bfloat16 [8, 128, 16, 8, 1536], P('fsdp', 'tm', 'height'), may hold values from -6 to 6
- value_tangent: bfloat16 [8, 128, 16, 8, 1536], P('fsdp', 'tm', 'height'), may hold values from -6 to 6
- out_weight: bfloat16 [1536, 1536], P(None, ('height', 'fsdp')), may hold values from -0.15625 to 0.15625
- gate_table: float32 [64, 1536], replicated, may hold values from 0.5 to 1.5
- gate_slope: float32 [64, 1536], replicated, may hold values from -4 to 4
- timestep: int32 [8], P('fsdp'), may hold values from 0 to 63
Outputs:
- output_primal: bfloat16 [8, 128, 16, 8, 1536], P('fsdp', 'tm', 'height')
- output_tangent: bfloat16 [8, 128, 16, 8, 1536], P('fsdp', 'tm', 'height')
All inputs are finite; a program needn't handle non-finite values.
Results may differ from a plain program's by a relative error of at most 0.008.
Values may be sent and summed in bfloat16 or wider, within the bound.
A program may use at most 64 MiB of HBM per device.

v0:
```python
import math

import jax
import jax.numpy as jnp
from jax import lax
from jax.sharding import PartitionSpec as P

HD = 128


def partner_2(value, axis, apart):
    mask = 2**apart
    pairs = [(source, source ^ mask) for source in range(lax.axis_size(axis))]
    return lax.ppermute(value, axis, pairs)


def with_halo(x, sides, width):
    for axis, dim in sides:
        devices, length = (lax.axis_size(axis), x.shape[dim])
        up = [(i, (i + 1) % devices) for i in range(devices - 1)]
        down = [(j, i) for i, j in up]
        last = lax.slice_in_dim(x, length - width, length, axis=dim)
        first = lax.slice_in_dim(x, 0, width, axis=dim)
        before = lax.ppermute(last, axis, up)
        after = lax.ppermute(first, axis, down)
        x = jnp.concatenate([before, x, after], axis=dim)
    return x


def attend(queries, keys_all, values_all, queries_t, keys_t, values_t, allowed):
    scaling = 1.0 / math.sqrt(queries.shape[-1])
    scores = (
        jnp.einsum("qhd,khd->hqk", queries, keys_all, preferred_element_type=jnp.float32) * scaling
    )
    scores = jnp.where(allowed[None], scores, -1e30)
    row_max = jnp.max(scores, axis=-1, keepdims=True)
    lifted = jnp.exp(scores - row_max)
    probs = lifted / jnp.sum(lifted, axis=-1, keepdims=True)
    probs_low = probs.astype(jnp.bfloat16)
    primal = jnp.einsum("hqk,khd->qhd", probs_low, values_all, preferred_element_type=jnp.float32)
    joined_q = jnp.concatenate([queries_t, queries], 2)
    joined_k = jnp.concatenate([keys_all, keys_t], 2)
    slopes = (
        jnp.einsum("qhd,khd->hqk", joined_q, joined_k, preferred_element_type=jnp.float32) * scaling
    )
    centre = jnp.sum(probs * slopes, axis=-1, keepdims=True)
    weights_t = (probs * (slopes - centre)).astype(jnp.bfloat16)
    joined_w = jnp.concatenate([weights_t, probs_low], 2)
    joined_v = jnp.concatenate([values_all, values_t], 0)
    tangent = jnp.einsum("hqk,khd->qhd", joined_w, joined_v, preferred_element_type=jnp.float32)
    return (primal.astype(jnp.bfloat16), tangent.astype(jnp.bfloat16))


def finish(stacked, weight_block, gate_part, slope_part):
    pair_count, token_count, features = stacked.shape
    both = jnp.dot(
        stacked.reshape(pair_count * token_count, features),
        weight_block,
        preferred_element_type=jnp.float32,
    ).reshape(pair_count, token_count, -1)
    out_p = (gate_part * both[0]).astype(jnp.bfloat16)
    out_t = (gate_part * both[1] + slope_part * both[0]).astype(jnp.bfloat16)
    return jnp.stack([out_p, out_t])


def local(
    query_primal,
    key_primal,
    value_primal,
    query_tangent,
    key_tangent,
    value_tangent,
    out_weight,
    gate_table,
    gate_slope,
    timestep,
):
    frames_dev = query_primal.shape[1]
    rows_dev = query_primal.shape[2]
    columns = query_primal.shape[3]
    features = query_primal.shape[4]
    head_count = features // HD
    packed = jnp.stack([key_primal, value_primal, key_tangent, value_tangent])[:, 0]
    partner = partner_2(packed, "height", 0)
    lower_half = lax.axis_index("height") % 2 == 0
    tile_block = jnp.where(
        lower_half, jnp.concatenate([packed, partner], 2), jnp.concatenate([partner, packed], 2)
    )
    extended = with_halo(tile_block, (("tm", 1),), 1)
    ext_frames = frames_dev + 2
    key_sets = extended.reshape(4, -1, head_count, HD)
    frame_ids = lax.broadcasted_iota(jnp.int32, (ext_frames, 2 * rows_dev, columns), 0).reshape(-1)
    global_frame = lax.axis_index("tm") * frames_dev + frame_ids - 1
    total_frames = frames_dev * lax.axis_size("tm")
    inside = (global_frame >= 0) & (global_frame < total_frames)
    allowed = inside[None, :]
    query_flat = query_primal.reshape(-1, head_count, HD)
    query_flat_t = query_tangent.reshape(-1, head_count, HD)
    primal, tangent = attend(
        query_flat, key_sets[0], key_sets[1], query_flat_t, key_sets[2], key_sets[3], allowed
    )
    token_count = query_flat.shape[0]
    stacked = jnp.stack(
        [primal.reshape(token_count, features), tangent.reshape(token_count, features)]
    )
    step_total = gate_table.shape[0]
    chosen = lax.broadcasted_iota(jnp.int32, (step_total, 1), 0) == timestep[0]
    gate_row = jnp.sum(jnp.where(chosen, gate_table, 0.0), axis=0)
    slope_row = jnp.sum(jnp.where(chosen, gate_slope, 0.0), axis=0)
    result = finish(
        stacked,
        lax.all_gather(out_weight, ("height", "fsdp"), axis=1, tiled=True),
        gate_row,
        slope_row,
    )
    dout = result.shape[2]
    out_p = result[0].reshape(1, frames_dev, rows_dev, columns, dout)
    out_t = result[1].reshape(1, frames_dev, rows_dev, columns, dout)
    return (out_p, out_t)


def solution(mesh):
    in_specs = (
        P("fsdp", "tm", "height", None, None),
        P("fsdp", "tm", "height", None, None),
        P("fsdp", "tm", "height", None, None),
        P("fsdp", "tm", "height", None, None),
        P("fsdp", "tm", "height", None, None),
        P("fsdp", "tm", "height", None, None),
        P(None, ("height", "fsdp")),
        P(),
        P(),
        P("fsdp"),
    )
    out_specs = (P("fsdp", "tm", "height", None, None), P("fsdp", "tm", "height", None, None))
    return jax.shard_map(local, mesh=mesh, in_specs=in_specs, out_specs=out_specs, check_vma=False)
```

profile of v0, /device:TPU:78, one launch (start us, length us, event | category | flops | bytes accessed | tf_op | source)
XLA Modules:
  0.0 221.8 jit_solution(4385341056181969781)
XLA Ops:
  7.2 0.0 all-gather.2.cloned.1.call-start
  7.2 0.7 all-gather.2.cloned.1.call-update
  7.9 1.5 maximum_bitcast_fusion
  9.5 0.0 copy-start
  9.5 2.7 %collective-permute-start = (bf16[4,4,4,8,1536]{4,3,2,1,0:T(8,128)(2,1)S(1)}, bf16[4,4,4,8,1536]{4,3,2,1,0:T(8,128)(2,1)}, u32[]{:S(2)}, u32[]{:S(2)}) collective-permute-start(bf16[4,4,4,8,1536]{4,3,2,1,0:T(8,128)(2,1)S(1)} %maximum_bitcast_fusion), channel_id=1, source_target_pairs={{0,8},{8,0},{16,24},{24,16},{1,9},{9,1},{17,25},{25,17},{2,10},{10... | collective-permute-start | bytes 4718600 | tf_op jit(solution)/shard_map/ppermute | solution.py:14
  12.2 0.0 copy-done
  12.2 38.8 %collective-permute-done = bf16[4,4,4,8,1536]{4,3,2,1,0:T(8,128)(2,1)} collective-permute-done((bf16[4,4,4,8,1536]{4,3,2,1,0:T(8,128)(2,1)S(1)}, bf16[4,4,4,8,1536]{4,3,2,1,0:T(8,128)(2,1)}, u32[]{:S(2)}, u32[]{:S(2)}) %collective-permute-start) | collective-permute-done | bytes 1572896 | tf_op jit(solution)/shard_map/ppermute | solution.py:14
  51.0 3.4 %maximum_select_fusion = bf16[4,4,8,8,1536]{4,3,2,1,0:T(8,128)(2,1)S(1)} fusion(bf16[4,4,4,8,1536]{4,3,2,1,0:T(8,128)(2,1)} %collective-permute-done, bf16[4,4,4,8,1536]{4,3,2,1,0:T(8,128)(2,1)} %copy-done, pred[]{:T(512)S(6)} %eq.18), kind=kLoop, calls=%fused_computation.3 | loop fusion | flops 4718592 | bytes 6291457 | tf_op jit(solution)/shard_map/jit(_where)/select_n | solution.py:86
  54.3 0.0 copy-start.5
  54.4 1.3 fusion.47
  55.7 1.9 collective-permute-start.2
  57.6 3.3 %collective-permute-start.1 = (bf16[4,1,8,8,1536]{4,3,2,1,0:T(8,128)(2,1)}, bf16[4,1,8,8,1536]{4,3,2,1,0:T(8,128)(2,1)}, u32[]{:S(2)}, u32[]{:S(2)}) collective-permute-start(bf16[4,1,8,8,1536]{4,3,2,1,0:T(8,128)(2,1)} %get-tuple-element.8), channel_id=1, source_target_pairs={{0,32},{32,64},{64,96},{96,128},{128,160},{160,192},{192,224},{224... | collective-permute-start | bytes 2359304 | tf_op jit(solution)/shard_map/ppermute | solution.py:24
  60.9 0.6 and.19
  61.5 0.0 copy-done.5
  61.5 1.1 reshape.56
  62.7 1.1 copy.18
  63.8 0.0 copy-start.6
  63.8 2.3 %reshape.57 = bf16[128,12,128]{2,1,0:T(8,128)(2,1)} reshape(bf16[1,4,4,8,1536]{4,3,2,1,0:T(8,128)(2,1)} %param.13) | data formatting | bytes 786432 | tf_op jit(solution)/shard_map/reshape | solution.py:98
  66.1 1.9 copy.23
  68.6 1.3 select_reduce_fusion
  69.9 0.0 collective-permute-done.2
  69.9 1.3 collective-permute-done.1
  71.2 1.7 pad_maximum_fusion
  73.0 1.9 fusion.46
  74.9 2.5 %squeeze.24 = bf16[384,12,128]{2,1,0:T(8,128)(2,1)S(1)} reshape(bf16[1,6,8,8,1536]{4,3,2,1,0:T(8,128)(2,1)} %get-tuple-element.7) | data formatting | bytes 2359296 | tf_op jit(solution)/shard_map/squeeze | solution.py:100
  77.4 1.4 copy.17
  78.8 2.5 %squeeze.26 = bf16[384,12,128]{2,1,0:T(8,128)(2,1)S(1)} reshape(bf16[1,6,8,8,1536]{4,3,2,1,0:T(8,128)(2,1)} %get-tuple-element.5) | data formatting | bytes 2359296 | tf_op jit(solution)/shard_map/squeeze | solution.py:100
  81.3 1.3 copy.26
  82.6 2.5 %squeeze.25 = bf16[384,12,128]{2,1,0:T(8,128)(2,1)S(1)} reshape(bf16[1,6,8,8,1536]{4,3,2,1,0:T(8,128)(2,1)} %get-tuple-element.6) | data formatting | bytes 2359296 | tf_op jit(solution)/shard_map/squeeze | solution.py:100
  85.1 1.9 copy.22
  87.0 0.0 copy-start.7
  87.0 0.8 squeeze.23
  87.9 0.0 copy-start.3
  87.9 1.9 copy.19
  89.8 0.0 copy-done.6
  89.8 0.0 copy-done.7
  89.8 0.0 copy-done.3
  89.8 3.5 %fusion.6 = f32[12,128,384]{1,2,0:T(8,128)} fusion(bf16[384,12,128]{2,0,1:T(8,128)(2,1)} %copy.26, bf16[384,12,128]{2,0,1:T(8,128)(2,1)S(1)} %copy-done.3, bf16[128,12,128]{2,0,1:T(8,128)(2,1)S(1)} %copy.18, bf16[128,12,128]{2,0,1:T(8,128)(2,1)S(1)} %copy-done.7), kind=kOutput, calls=%fused_computation.8 | convolution fusion | flops 308281344 | bytes 5505024 | tf_op jit(solution)/shard_map/qhd,khd->hqk/dot_general | solution.py:44
  93.2 2.5 %fusion.48 = (f32[12,128]{1,0:T(8,128)}, f32[12,128,384]{1,2,0:T(8,128)S(1)}) fusion(pred[384]{0:T(512)(128)(4,1)} %and.19, bf16[384,12,128]{2,0,1:T(8,128)(2,1)S(1)} %copy-done.3, bf16[128,12,128]{2,0,1:T(8,128)(2,1)} %copy-done.6), kind=kOutput, calls=%fused_computation.56 | convolution fusion | flops 153354624 | bytes 3938688 | tf_op jit(solution)/shard_map/sub | solution.py:37
  95.7 0.0 copy-start.2
  95.7 0.0 copy-start.8
  95.7 0.0 copy-start.9
  95.7 1.5 copy-done.2
  97.2 1.1 fusion.45
  98.3 0.0 copy-done.8
  98.3 0.0 copy-done.9
  98.3 0.0 copy-start.1
  98.3 0.0 copy-start.4
  98.3 3.4 %multiply_convert_fusion = bf16[12,128,384]{1,2,0:T(8,128)(2,1)S(1)} fusion(f32[12,128,384]{1,2,0:T(8,128)S(1)} %copy-done.9, f32[12,128,384]{1,2,0:T(8,128)} %copy-done.2, f32[12,128]{1,0:T(8,128)S(1)} %copy-done.8), kind=kOutput, calls=%fused_computation.19 | output fusion | flops 4720511 | bytes 5904384 | tf_op jit(solution)/shard_map/sub | solution.py:47
  101.7 0.0 copy-done.1
  101.7 0.0 copy-done.4
  101.7 0.8 fusion.21
  102.5 0.2 copy.30
  102.7 0.5 convolution_convert_fusion
  103.2 0.2 copy.29
  103.4 0.1 pad_maximum_fusion.1
  103.5 106.7 %all-gather.2.cloned.1.call-done = bf16[1536,1536]{0,1:T(8,128)(2,1)} async-done(((bf16[1536,48]{0,1:T(8,128)(2,1)}), bf16[1536,1536]{0,1:T(8,128)(2,1)}) %all-gather.2.cloned.1.call-update) | async-done | bytes 4718608 | tf_op jit(solution)/shard_map/all_gather | solution.py:112
  210.1 3.7 %fusion.49 = f32[256,1536]{1,0:T(8,128)S(1)} fusion(bf16[256,1536]{1,0:T(8,128)(2,1)S(1)} %bitcast.49, bf16[1536,1536]{0,1:T(8,128)(2,1)} %all-gather.2.cloned.1.call-done), kind=kOutput, calls=%fused_computation.57 | convolution fusion | flops 1207959552 | bytes 7077888 | tf_op jit(solution)/shard_map/dot_general | solution.py:56
  213.9 1.0 fusion.31
  (2 shorter events, 0.0 us)
Async XLA Ops:
  7.2 203.0 %all-gather.2.cloned.1.call-start = ((), (), s32[]{:S(2)}) async-start(), calls=%async_computation | async-start | bytes 4866048 | tf_op jit(solution)/shard_map/all_gather | solution.py:112
  9.5 2.7 %copy-start = (bf16[4,4,4,8,1536]{4,3,2,1,0:T(8,128)(2,1)}, bf16[4,4,4,8,1536]{4,3,2,1,0:T(8,128)(2,1)S(1)}, u32[]{:S(2)}) copy-start(bf16[4,4,4,8,1536]{4,3,2,1,0:T(8,128)(2,1)S(1)} %maximum_bitcast_fusion) | copy-start | bytes 4718596
  9.5 41.5 %collective-permute-start = (bf16[4,4,4,8,1536]{4,3,2,1,0:T(8,128)(2,1)S(1)}, bf16[4,4,4,8,1536]{4,3,2,1,0:T(8,128)(2,1)}, u32[]{:S(2)}, u32[]{:S(2)}) collective-permute-start(bf16[4,4,4,8,1536]{4,3,2,1,0:T(8,128)(2,1)S(1)} %maximum_bitcast_fusion), channel_id=1, source_target_pairs={{0,8},{8,0},{16,24},{24,16},{1,9},{9,1},{17,25},{25,17},{2,10},{10... | collective-permute-start | bytes 4718600 | tf_op jit(solution)/shard_map/ppermute | solution.py:14
  54.3 7.2 %copy-start.5 = (bf16[1,4,4,8,1536]{4,3,2,1,0:T(8,128)(2,1)S(1)}, bf16[1,4,4,8,1536]{4,3,2,1,0:T(8,128)(2,1)}, u32[]{:S(2)}) copy-start(bf16[1,4,4,8,1536]{4,3,2,1,0:T(8,128)(2,1)} %param.10) | copy-start | bytes 1179652
  55.7 14.2 %collective-permute-start.2 = (bf16[4,1,8,8,1536]{4,3,2,1,0:T(8,128)(2,1)}, bf16[4,1,8,8,1536]{4,3,2,1,0:T(8,128)(2,1)}, u32[]{:S(2)}, u32[]{:S(2)}) collective-permute-start(bf16[4,1,8,8,1536]{4,3,2,1,0:T(8,128)(2,1)} %get-tuple-element.9), channel_id=1, source_target_pairs={{32,0},{64,32},{96,64},{128,96},{160,128},{192,160},{224,192},{256... | collective-permute-start | bytes 2359304 | tf_op jit(solution)/shard_map/ppermute | solution.py:25
  57.6 13.6 %collective-permute-start.1 = (bf16[4,1,8,8,1536]{4,3,2,1,0:T(8,128)(2,1)}, bf16[4,1,8,8,1536]{4,3,2,1,0:T(8,128)(2,1)}, u32[]{:S(2)}, u32[]{:S(2)}) collective-permute-start(bf16[4,1,8,8,1536]{4,3,2,1,0:T(8,128)(2,1)} %get-tuple-element.8), channel_id=1, source_target_pairs={{0,32},{32,64},{64,96},{96,128},{128,160},{160,192},{192,224},{224... | collective-permute-start | bytes 2359304 | tf_op jit(solution)/shard_map/ppermute | solution.py:24
  63.8 26.0 %copy-start.6 = (bf16[128,12,128]{2,0,1:T(8,128)(2,1)}, bf16[128,12,128]{2,0,1:T(8,128)(2,1)S(1)}, u32[]{:S(2)}) copy-start(bf16[128,12,128]{2,0,1:T(8,128)(2,1)S(1)} %copy.18) | copy-start | bytes 1179652
  87.0 2.8 %copy-start.7 = (bf16[128,12,128]{2,0,1:T(8,128)(2,1)S(1)}, bf16[128,12,128]{2,0,1:T(8,128)(2,1)}, u32[]{:S(2)}) copy-start(bf16[128,12,128]{2,0,1:T(8,128)(2,1)} %copy.23) | copy-start | bytes 1179652
  87.9 1.9 copy-start.3
  95.7 1.5 copy-start.2
  95.7 2.5 %copy-start.8 = (f32[12,128]{1,0:T(8,128)S(1)}, f32[12,128]{1,0:T(8,128)}, u32[]{:S(2)}) copy-start(f32[12,128]{1,0:T(8,128)} %get-tuple-element.12) | copy-start | bytes 18436
  95.7 2.5 %copy-start.9 = (f32[12,128,384]{1,2,0:T(8,128)S(1)}, f32[12,128,384]{1,2,0:T(8,128)}, u32[]{:S(2)}) copy-start(f32[12,128,384]{1,2,0:T(8,128)} %fusion.6) | copy-start | bytes 7077892
  98.3 3.4 %copy-start.1 = (bf16[384,12,128]{0,2,1:T(8,128)(2,1)S(1)}, bf16[384,12,128]{0,2,1:T(8,128)(2,1)}, u32[]{:S(2)}) copy-start(bf16[384,12,128]{0,2,1:T(8,128)(2,1)} %copy.19) | copy-start | bytes 3538948
  98.3 3.4 %copy-start.4 = (bf16[384,12,128]{0,2,1:T(8,128)(2,1)S(1)}, bf16[384,12,128]{0,2,1:T(8,128)(2,1)}, u32[]{:S(2)}) copy-start(bf16[384,12,128]{0,2,1:T(8,128)(2,1)} %copy.22) | copy-start | bytes 3538948
Sparse Core Ops, SparseCore 0:
  10.7 199.4 all-gather.1
where the time goes:
time: 222 us
  waiting for transfers between devices  147 us (66%)
  local copies, waits for them, and re-layouts  27 us (12%)
  between operations  15 us (7%)
  other arithmetic  13.5 us (6%)
  matrix products  11 us (5%)
  starting transfers between devices  7.93 us (4%)
    all_gather x1, waiting for transfers between devices, local(): lax.all_gather(out_weight, ('height', 'fsdp'), axis=1, tiled=True)  107 us
    ppermute x1, waiting for transfers between devices, partner_2(): return lax.ppermute(value, axis, pairs)  38.8 us
  transfers between devices with their start and end apart: 4, of which 3 were waited for; matrix products, arithmetic and copies ran while one was open for 20% of the time, Pallas kernels for 0%

commit v1 on v0

v1 whole, which is shorter than its diff:
```python
import functools
import math

import jax
import jax.numpy as jnp
from jax import lax
from jax.experimental import pallas as pl
from jax.experimental.pallas import tpu as pltpu
from jax.sharding import PartitionSpec as P

HD = 128
PAIR = 2
MESH = pl.DeviceIdType.MESH
NT = (((1,), (1,)), ((), ()))


def kernel(
    dims,
    step_ref,
    q_ref,
    k_ref,
    v_ref,
    qt_ref,
    kt_ref,
    vt_ref,
    w_ref,
    gate_ref,
    slope_ref,
    outp_ref,
    outt_ref,
    kv,
    qq,
    attn,
    wbuf,
    gates,
    load_sem,
    part_s,
    part_r,
    ownl_s,
    ownl_r,
    ownr_s,
    ownr_r,
    rell_s,
    rell_r,
    relr_s,
    relr_r,
    ws,
    wr,
):
    n_tm, n_h, n_z, tokens, frame, features, shard = dims
    chunks = features // (PAIR * HD)
    wide = PAIR * HD
    khalf = features // 2
    half_tm = n_tm // 2
    tm = lax.axis_index("tm")
    h = lax.axis_index("height")
    z = lax.axis_index("fsdp")
    core = lax.rem(tm, 2)
    twin = h + 1 - 2 * lax.rem(h, 2)
    partner = (tm, twin, z)
    outer = jnp.logical_or(h == 0, h == n_h - 1)
    gap = (jnp.where(outer, lax.rem(tm + half_tm, n_tm), tm), n_h - 1 - h, z)
    z_up = lax.rem(z + 1, n_z)
    z_down = lax.rem(z + n_z - 1, n_z)
    above = (tm, h, z_up)
    below = (tm, h, z_down)
    left = (tm - 1, h, z)
    right = (tm + 1, h, z)
    sibling = (tm + 1 - 2 * core, h, z)
    has_left = tm > 0
    has_right = tm < n_tm - 1
    cross_left = tm == half_tm
    cross_right = tm == half_tm - 1

    own = 0
    other = tokens
    left_own = 2 * tokens
    left_other = left_own + frame
    right_own = left_other + frame
    right_other = right_own + frame
    last = tokens - frame

    barrier = pltpu.get_barrier_semaphore()
    for peer in (partner, gap, above, below):
        pl.semaphore_signal(barrier, inc=1, device_id=peer, device_id_type=MESH)

    @pl.when(has_left)
    def _():
        pl.semaphore_signal(barrier, inc=1, device_id=left, device_id_type=MESH)

    @pl.when(has_right)
    def _():
        pl.semaphore_signal(barrier, inc=1, device_id=right, device_id_type=MESH)

    kv_loads = [
        pltpu.make_async_copy(ref, kv.at[i, pl.ds(own, tokens)], load_sem.at[i])
        for i, ref in enumerate((k_ref, v_ref, kt_ref, vt_ref))
    ]
    q_loads = [
        pltpu.make_async_copy(ref, qq.at[i], load_sem.at[4 + i])
        for i, ref in enumerate((q_ref, qt_ref))
    ]
    gate_loads = [
        pltpu.make_async_copy(ref, gates.at[i], load_sem.at[6 + i])
        for i, ref in enumerate((gate_ref, slope_ref))
    ]
    columns = pl.ds(pl.multiple_of(core * khalf, HD), khalf)

    def shard_of(height):
        return wbuf.at[core, z, pl.ds(pl.multiple_of(height * shard, 16), shard)]

    w_load = pltpu.make_async_copy(w_ref.at[:, columns], shard_of(h), load_sem.at[8])
    w_load.start()
    for copy in kv_loads + q_loads + gate_loads:
        copy.start()

    rows = 2 * frame

    @pl.when(jnp.logical_not(has_left))
    def _():
        kv[:, pl.ds(left_own, rows), :] = jnp.zeros((4, rows, features), kv.dtype)

    @pl.when(jnp.logical_not(has_right))
    def _():
        kv[:, pl.ds(right_own, rows), :] = jnp.zeros((4, rows, features), kv.dtype)

    w_load.wait()
    for copy in kv_loads:
        copy.wait()
    peers = 4 + has_left.astype(jnp.int32) + has_right.astype(jnp.int32)
    pl.semaphore_wait(barrier, peers)

    def move(source, target, send, recv, device):
        return pltpu.make_async_remote_copy(
            src_ref=source,
            dst_ref=target,
            send_sem=send,
            recv_sem=recv,
            device_id=device,
            device_id_type=MESH,
        )

    def block(row, count, g):
        cols = pl.ds(pl.multiple_of(g * wide, wide), wide)
        return kv.at[:, pl.ds(row, count), cols]

    def to_partner(g):
        return move(block(own, tokens, g), block(other, tokens, g), part_s.at[g], part_r.at[g], partner)

    def own_left(g):
        return move(block(own, frame, g), block(right_own, frame, g), ownl_s.at[g], ownr_r.at[g], left)

    def own_right(g):
        return move(block(last, frame, g), block(left_own, frame, g), ownr_s.at[g], ownl_r.at[g], right)

    def relay_left(g):
        return move(block(other, frame, g), block(right_other, frame, g), rell_s.at[g], relr_r.at[g], left)

    def relay_right(g):
        return move(block(other + last, frame, g), block(left_other, frame, g), relr_s.at[g], rell_r.at[g], right)

    def cross_to_left(g):
        return move(block(left_own, frame, g), block(left_other, frame, g), rell_s.at[g], rell_r.at[g], partner)

    def cross_to_right(g):
        return move(block(right_own, frame, g), block(right_other, frame, g), relr_s.at[g], relr_r.at[g], partner)

    def shard_move(height, slot, device):
        return move(shard_of(height), shard_of(height), ws.at[slot], wr.at[slot], device)

    to_p = shard_move(h, 0, partner)
    to_g = shard_move(h, 1, gap)
    on_g = shard_move(twin, 2, gap)

    def z_block(which, parts):
        block_rows = n_h * shard
        first, count = (0, block_rows)
        if parts == 1:
            count = block_rows // 2
        if parts == 2:
            first = count = block_rows // 2
        return wbuf.at[core, which, pl.ds(first, count)]

    hops = n_z // 2

    def ring_up(step):
        ref = z_block(lax.rem(z + n_z - step, n_z), 1 if step == hops - 1 else 0)
        return move(ref, ref, ws.at[3 + step], wr.at[3 + step], above)

    def ring_down(step):
        ref = z_block(lax.rem(z + step, n_z), 2 if step == hops - 1 else 0)
        return move(ref, ref, ws.at[3 + hops + step], wr.at[3 + hops + step], below)

    def across(offset):
        ref = wbuf.at[core, lax.rem(z + offset, n_z)]
        slot = 3 + 2 * hops + offset
        return move(ref, ref, ws.at[slot], wr.at[slot], sibling)

    to_p.start()
    to_g.start()
    to_partner(0).start()
    to_partner(1).start()

    def send_own(g, carry):
        @pl.when(has_left)
        def _():
            own_left(g).start()

        @pl.when(has_right)
        def _():
            own_right(g).start()

        return carry

    lax.fori_loop(0, chunks, send_own, 0)

    to_p.wait_recv()
    on_g.start()
    to_g.wait_recv()
    on_g.wait_recv()
    ring_up(0).start()
    ring_down(0).start()
    across(0).start()

    for copy in q_loads:
        copy.wait()

    scaling = 1.0 / math.sqrt(HD)
    spot = lax.broadcasted_iota(jnp.int32, (1, 4 * frame), 1)
    hidden = jnp.logical_or(
        jnp.logical_and(jnp.logical_not(has_left), spot < 2 * frame),
        jnp.logical_and(jnp.logical_not(has_right), spot >= 2 * frame),
    )
    bias = jnp.where(hidden, -1e30, 0.0).astype(jnp.float32)

    def attend(cols):
        q, qt = qq[0, :, cols], qq[1, :, cols]
        k, v, kt, vt = (kv[i, :, cols] for i in range(4))
        scores = lax.dot_general(q, k, NT, preferred_element_type=jnp.float32) * scaling
        scores = jnp.concatenate([scores[:, : 2 * tokens], scores[:, 2 * tokens :] + bias], 1)
        lifted = jnp.exp(scores - jnp.max(scores, axis=-1, keepdims=True))
        probs = lifted * (1.0 / jnp.sum(lifted, axis=-1, keepdims=True))
        low = probs.astype(jnp.bfloat16)
        slopes = (
            lax.dot_general(
                jnp.concatenate([qt, q], 1),
                jnp.concatenate([k, kt], 1),
                NT,
                preferred_element_type=jnp.float32,
            )
            * scaling
        )
        centre = jnp.sum(probs * slopes, axis=-1, keepdims=True)
        bent = (probs * (slopes - centre)).astype(jnp.bfloat16)
        primal = jnp.dot(low, v, preferred_element_type=jnp.float32)
        tangent = jnp.dot(bent, v, preferred_element_type=jnp.float32)
        tangent = tangent + jnp.dot(low, vt, preferred_element_type=jnp.float32)
        attn[pl.ds(0, tokens), cols] = primal.astype(jnp.bfloat16)
        attn[pl.ds(tokens, tokens), cols] = tangent.astype(jnp.bfloat16)

    def ring_stage(step):
        ring_up(step - 1).wait_recv()
        ring_down(step - 1).wait_recv()
        if step < hops:
            ring_up(step).start()
            ring_down(step).start()
            across(n_z - step).start()
            across(step).start()
        else:
            across(hops).start()

    def chunk(g, carry):
        to_partner(g).wait_recv()

        @pl.when(jnp.logical_and(has_left, jnp.logical_not(cross_left)))
        def _():
            relay_left(g).start()

        @pl.when(jnp.logical_and(has_right, jnp.logical_not(cross_right)))
        def _():
            relay_right(g).start()

        @pl.when(g < chunks - 2)
        def _():
            to_partner(g + 2).start()

        for step in range(1, hops + 1):

            @pl.when(g == step)
            def _():
                ring_stage(step)

        @pl.when(has_left)
        def _():
            own_right(g).wait_recv()

        @pl.when(cross_left)
        def _():
            cross_to_left(g).start()

        @pl.when(has_right)
        def _():
            own_left(g).wait_recv()

        @pl.when(cross_right)
        def _():
            cross_to_right(g).start()

        @pl.when(has_left)
        def _():
            relay_right(g).wait_recv()

        @pl.when(has_right)
        def _():
            relay_left(g).wait_recv()

        for head in range(PAIR):
            attend(pl.ds(pl.multiple_of(g * wide + head * HD, HD), HD))
        return carry

    lax.fori_loop(0, chunks, chunk, 0)

    for copy in gate_loads:
        copy.wait()
    for offset in range(n_z):
        across(offset).wait_recv()

    which = step_ref[0]
    gate_row = gates[0, pl.ds(which, 1), :]
    slope_row = gates[1, pl.ds(which, 1), :]
    span = n_z * shard
    for height in range(n_h):
        outs = slice(height * span, (height + 1) * span)
        both = None
        for part in range(2):
            weight = jnp.concatenate(
                [wbuf[part, i, height * shard : (height + 1) * shard, :] for i in range(n_z)], 0
            )
            term = lax.dot_general(
                attn[:, part * khalf : (part + 1) * khalf],
                weight,
                NT,
                preferred_element_type=jnp.float32,
            )
            both = term if both is None else both + term
        gate = gate_row[:, outs]
        outp_ref[:, outs] = (gate * both[:tokens]).astype(outp_ref.dtype)
        tangent = gate * both[tokens:] + slope_row[:, outs] * both[:tokens]
        outt_ref[:, outs] = tangent.astype(outt_ref.dtype)

    def finish(g, carry):
        to_partner(g).wait_send()

        @pl.when(has_left)
        def _():
            own_left(g).wait_send()
            relay_left(g).wait_send()

        @pl.when(has_right)
        def _():
            own_right(g).wait_send()
            relay_right(g).wait_send()

        return carry

    lax.fori_loop(0, chunks, finish, 0)
    to_p.wait_send()
    to_g.wait_send()
    on_g.wait_send()
    for step in range(hops):
        ring_up(step).wait_send()
        ring_down(step).wait_send()
    for offset in range(n_z):
        across(offset).wait_send()


def local(sizes, q, k, v, qt, kt, vt, weight, gate_table, gate_slope, timestep):
    _, frames, rows, cols, features = q.shape
    tokens = frames * rows * cols
    frame = rows * cols
    shard = weight.shape[1]
    n_tm, n_h, n_z = sizes
    chunks = features // (PAIR * HD)
    flat = [a.reshape(tokens, features) for a in (q, k, v, qt, kt, vt)]
    steps = gate_table.shape[0]
    dma = pltpu.SemaphoreType.DMA
    dims = (n_tm, n_h, n_z, tokens, frame, features, shard)
    weights = 3 + n_z + n_z
    anywhere = pl.BlockSpec(memory_space=pl.ANY)
    out = jax.ShapeDtypeStruct((tokens, features), jnp.bfloat16)
    out_p, out_t = pl.pallas_call(
        functools.partial(kernel, dims),
        out_shape=(out, out),
        in_specs=[pl.BlockSpec(memory_space=pltpu.SMEM)] + [anywhere] * 9,
        out_specs=(pl.BlockSpec(memory_space=pltpu.VMEM),) * 2,
        scratch_shapes=[
            pltpu.VMEM((4, 2 * tokens + 4 * frame, features), jnp.bfloat16),
            pltpu.VMEM((2, tokens, features), jnp.bfloat16),
            pltpu.VMEM((2 * tokens, features), jnp.bfloat16),
            pltpu.VMEM((2, n_z, n_h * shard, features // 2), jnp.bfloat16),
            pltpu.VMEM((2, steps, features), jnp.float32),
            dma((9,)),
        ]
        + [dma((chunks,))] * 10
        + [dma((weights,))] * 2,
        compiler_params=pltpu.CompilerParams(collective_id=0, has_side_effects=True),
        name="tiled_attention",
    )(timestep, *flat, weight.T, gate_table, gate_slope)
    return (out_p.reshape(q.shape), out_t.reshape(q.shape))


def solution(mesh):
    spec = P("fsdp", "tm", "height", None, None)
    in_specs = (spec,) * 6 + (P(None, ("height", "fsdp")), P(None, None), P(None, None), P("fsdp"))
    sizes = (mesh.shape["tm"], mesh.shape["height"], mesh.shape["fsdp"])
    return jax.shard_map(
        functools.partial(local, sizes),
        mesh=mesh,
        in_specs=in_specs,
        out_specs=(spec, spec),
        check_vma=False,
    )
```

time: 222 us -> 85.5 us (0.39)
  the two profiles are of different devices: /device:TPU:78 before, /device:TPU:112 now
where the time goes in v1:
time: 85.5 us; the launch traced here: 85.3 us
  Pallas kernels  81.5 us (95%)
  local copies, waits for them, and re-layouts  2.57 us (3%)
  between operations  1.3 us (2%)
    pallas_call x1, Pallas kernels, local(): pl.pallas_call(functools.partial(kernel, dims), out_shape=(out, out), in_...  81.5 us
    unnamed x4, local copies, waits for them, and re-layouts  2.57 us

profile of v1, /device:TPU:112, one launch (start us, length us, event | category | flops | bytes accessed | tf_op | source)
XLA Modules:
  0.0 85.3 jit_solution(5138028966276799432)
XLA Ops:
  1.3 81.5 %tiled_attention.1 = (bf16[128,1536]{1,0:T(8,128)(2,1)}, bf16[128,1536]{1,0:T(8,128)(2,1)}) custom-call(s32[1]{0:T(128)S(6)} %copy.14.step_ref, bf16[128,1536]{1,0:T(8,128)(2,1)} %bitcast.11, bf16[128,1536]{1,0:T(8,128)(2,1)} %bitcast.12, bf16[128,1536]{1,0:T(8,128)(2,1)} %bitcast.13, bf16[128,1536]{1,0:T(8,128)(2,1)} %bitcast.14, ...), custom_call_target="tpu_custom_call" | custom-call | tf_op jit(solution)/shard_map/tiled_attention/pallas_call | solution.py:391
  82.8 0.0 copy-start
  82.8 1.8 %copy.15 = bf16[1,4,4,8,1536]{4,3,2,1,0:T(8,128)(2,1)} copy(bf16[1,4,4,8,1536]{4,3,2,1,0:T(8,128)(2,1)} %bitcast.10) | data formatting | bytes 786432
  84.6 0.0 copy-done
  84.6 0.7 copy.16
Async XLA Ops:
  82.8 1.8 %copy-start = (bf16[128,1536]{1,0:T(8,128)(2,1)S(1)}, bf16[128,1536]{1,0:T(8,128)(2,1)}, u32[]{:S(2)}) copy-start(bf16[128,1536]{1,0:T(8,128)(2,1)} %get-tuple-element.5) | copy-start | bytes 1179652

commit v2 on v1

--- a/solution.py
+++ b/solution.py
@@ -33,6 +33,8 @@
     attn,
     wbuf,
     gates,
+    step_now,
+    hello,
     load_sem,
     part_s,
     part_r,
@@ -80,17 +82,33 @@
     right_other = right_own + frame
     last = tokens - frame
 
+    even = lax.rem(tm + h + z, 2) == 0
+    odd = jnp.logical_not(even)
     barrier = pltpu.get_barrier_semaphore()
-    for peer in (partner, gap, above, below):
-        pl.semaphore_signal(barrier, inc=1, device_id=peer, device_id_type=MESH)
-
-    @pl.when(has_left)
-    def _():
-        pl.semaphore_signal(barrier, inc=1, device_id=left, device_id_type=MESH)
-
-    @pl.when(has_right)
-    def _():
-        pl.semaphore_signal(barrier, inc=1, device_id=right, device_id_type=MESH)
+
+    def greet(semaphore):
+        for peer in (partner, gap):
+            pl.semaphore_signal(semaphore, inc=1, device_id=peer, device_id_type=MESH)
+
+        @pl.when(has_left)
+        def _():
+            pl.semaphore_signal(semaphore, inc=1, device_id=left, device_id_type=MESH)
+
+        @pl.when(has_right)
+        def _():
+            pl.semaphore_signal(semaphore, inc=1, device_id=right, device_id_type=MESH)
+
+    def greet_z(semaphore):
+        for peer in (above, below):
+            pl.semaphore_signal(semaphore, inc=1, device_id=peer, device_id_type=MESH)
+
+    @pl.when(even)
+    def _():
+        greet(barrier)
+
+    @pl.when(odd)
+    def _():
+        greet_z(barrier)
 
     kv_loads = [
         pltpu.make_async_copy(ref, kv.at[i, pl.ds(own, tokens)], load_sem.at[i])
@@ -110,8 +128,9 @@
         return wbuf.at[core, z, pl.ds(pl.multiple_of(height * shard, 16), shard)]
 
     w_load = pltpu.make_async_copy(w_ref.at[:, columns], shard_of(h), load_sem.at[8])
+    step_load = pltpu.make_async_copy(step_ref, step_now, load_sem.at[9])
     w_load.start()
-    for copy in kv_loads + q_loads + gate_loads:
+    for copy in kv_loads + q_loads + gate_loads + [step_load]:
         copy.start()
 
     rows = 2 * frame
@@ -123,12 +142,21 @@
     @pl.when(jnp.logical_not(has_right))
     def _():
         kv[:, pl.ds(right_own, rows), :] = jnp.zeros((4, rows, features), kv.dtype)
+
+    peers = 2 + has_left.astype(jnp.int32) + has_right.astype(jnp.int32)
+
+    @pl.when(odd)
+    def _():
+        pl.semaphore_wait(barrier, peers)
+        greet(hello.at[0])
+
+    @pl.when(even)
+    def _():
+        pl.semaphore_wait(hello.at[0], peers)
 
     w_load.wait()
     for copy in kv_loads:
         copy.wait()
-    peers = 4 + has_left.astype(jnp.int32) + has_right.astype(jnp.int32)
-    pl.semaphore_wait(barrier, peers)
 
     def move(source, target, send, recv, device):
         return pltpu.make_async_remote_copy(
@@ -172,34 +200,35 @@
     to_g = shard_move(h, 1, gap)
     on_g = shard_move(twin, 2, gap)
 
-    def z_block(which, parts):
-        block_rows = n_h * shard
-        first, count = (0, block_rows)
-        if parts == 1:
-            count = block_rows // 2
-        if parts == 2:
-            first = count = block_rows // 2
-        return wbuf.at[core, which, pl.ds(first, count)]
-
     hops = n_z // 2
-
-    def ring_up(step):
-        ref = z_block(lax.rem(z + n_z - step, n_z), 1 if step == hops - 1 else 0)
-        return move(ref, ref, ws.at[3 + step], wr.at[3 + step], above)
-
-    def ring_down(step):
-        ref = z_block(lax.rem(z + step, n_z), 2 if step == hops - 1 else 0)
-        return move(ref, ref, ws.at[3 + hops + step], wr.at[3 + hops + step], below)
+    half_rows = n_h * shard // 2
+
+    pair_row = pl.multiple_of(lax.div(h, 2) * half_rows, 16)
+    far_row = pl.multiple_of(half_rows - lax.div(h, 2) * half_rows, 16)
+
+    def z_block(which, sub):
+        return wbuf.at[core, which, pl.ds(far_row if sub else pair_row, half_rows)]
+
+    def ring_up(step, sub):
+        ref = z_block(lax.rem(z + n_z - step, n_z), sub)
+        slot = 3 + 2 * step + sub
+        return move(ref, ref, ws.at[slot], wr.at[slot], above)
+
+    def ring_down(step, sub):
+        ref = z_block(lax.rem(z + step, n_z), sub)
+        slot = 3 + 2 * hops + 2 * step + sub
+        return move(ref, ref, ws.at[slot], wr.at[slot], below)
 
     def across(offset):
         ref = wbuf.at[core, lax.rem(z + offset, n_z)]
-        slot = 3 + 2 * hops + offset
+        slot = 3 + 4 * hops + offset
         return move(ref, ref, ws.at[slot], wr.at[slot], sibling)
 
+    ahead = 3
     to_p.start()
     to_g.start()
-    to_partner(0).start()
-    to_partner(1).start()
+    for g in range(ahead):
+        to_partner(g).start()
 
     def send_own(g, carry):
         @pl.when(has_left)
@@ -216,11 +245,18 @@
 
     to_p.wait_recv()
     on_g.start()
-    to_g.wait_recv()
-    on_g.wait_recv()
-    ring_up(0).start()
-    ring_down(0).start()
-    across(0).start()
+
+    @pl.when(even)
+    def _():
+        pl.semaphore_wait(barrier, 2)
+        greet_z(hello.at[1])
+
+    @pl.when(odd)
+    def _():
+        pl.semaphore_wait(hello.at[1], 2)
+
+    ring_up(0, 0).start()
+    ring_down(0, 0).start()
 
     for copy in q_loads:
         copy.wait()
@@ -258,18 +294,36 @@
         attn[pl.ds(0, tokens), cols] = primal.astype(jnp.bfloat16)
         attn[pl.ds(tokens, tokens), cols] = tangent.astype(jnp.bfloat16)
 
-    def ring_stage(step):
-        ring_up(step - 1).wait_recv()
-        ring_down(step - 1).wait_recv()
-        if step < hops:
-            ring_up(step).start()
-            ring_down(step).start()
-            across(n_z - step).start()
-            across(step).start()
-        else:
-            across(hops).start()
-
-    def chunk(g, carry):
+    def ring_pass(step, sub):
+        ups = step < hops or sub == 0
+        downs = step < hops or sub == 1
+        if ups:
+            ring_up(step - 1, sub).wait_recv()
+        if downs:
+            ring_down(step - 1, sub).wait_recv()
+        if step < hops - 1 or (step == hops - 1 and sub == 0):
+            ring_up(step, sub).start()
+        if step < hops - 1 or (step == hops - 1 and sub == 1):
+            ring_down(step, sub).start()
+
+    def ring_stage(g):
+        if g == 0:
+            to_g.wait_recv()
+            on_g.wait_recv()
+            ring_up(0, 1).start()
+            ring_down(0, 1).start()
+            across(0).start()
+        if 1 <= g <= hops:
+            ring_pass(g, 1)
+            if g < hops:
+                across(n_z - g).start()
+                across(g).start()
+            else:
+                across(hops).start()
+        if g < hops:
+            ring_pass(g + 1, 0)
+
+    def forward(g):
         to_partner(g).wait_recv()
 
         @pl.when(jnp.logical_and(has_left, jnp.logical_not(cross_left)))
@@ -280,31 +334,40 @@
         def _():
             relay_right(g).start()
 
-        @pl.when(g < chunks - 2)
-        def _():
-            to_partner(g + 2).start()
-
-        for step in range(1, hops + 1):
-
-            @pl.when(g == step)
-            def _():
-                ring_stage(step)
-
-        @pl.when(has_left)
+        early = chunks // 2
+
+        @pl.when(g < 2)
+        def _():
+            for k in range(early):
+                other_chunk = g * early + k
+
+                @pl.when(cross_left)
+                def _():
+                    own_right(other_chunk).wait_recv()
+                    cross_to_left(other_chunk).start()
+
+                @pl.when(cross_right)
+                def _():
+                    own_left(other_chunk).wait_recv()
+                    cross_to_right(other_chunk).start()
+
+        @pl.when(g == 0)
+        def _():
+            for k in range(ahead, chunks - 1):
+                to_partner(k).start()
+
+        @pl.when(g == 1)
+        def _():
+            to_partner(chunks - 1).start()
+
+    def compute(g):
+        @pl.when(jnp.logical_and(has_left, jnp.logical_not(cross_left)))
         def _():
             own_right(g).wait_recv()
 
-        @pl.when(cross_left)
-        def _():
-            cross_to_left(g).start()
-
-        @pl.when(has_right)
+        @pl.when(jnp.logical_and(has_right, jnp.logical_not(cross_right)))
         def _():
             own_left(g).wait_recv()
-
-        @pl.when(cross_right)
-        def _():
-            cross_to_right(g).start()
 
         @pl.when(has_left)
         def _():
@@ -316,16 +379,33 @@
 
         for head in range(PAIR):
             attend(pl.ds(pl.multiple_of(g * wide + head * HD, HD), HD))
+
+    def chunk(g, carry):
+        @pl.when(g < chunks)
+        def _():
+            forward(g)
+
+        for stage in range(hops + 1):
+
+            @pl.when(g == stage)
+            def _():
+                ring_stage(stage)
+
+        @pl.when(g >= 1)
+        def _():
+            compute(g - 1)
+
         return carry
 
-    lax.fori_loop(0, chunks, chunk, 0)
-
+    lax.fori_loop(0, chunks + 1, chunk, 0)
+
+    step_load.wait()
     for copy in gate_loads:
         copy.wait()
     for offset in range(n_z):
         across(offset).wait_recv()
 
-    which = step_ref[0]
+    which = step_now[0]
     gate_row = gates[0, pl.ds(which, 1), :]
     slope_row = gates[1, pl.ds(which, 1), :]
     span = n_z * shard
@@ -368,8 +448,11 @@
     to_g.wait_send()
     on_g.wait_send()
     for step in range(hops):
-        ring_up(step).wait_send()
-        ring_down(step).wait_send()
+        for sub in range(2):
+            if step < hops - 1 or sub == 0:
+                ring_up(step, sub).wait_send()
+            if step < hops - 1 or sub == 1:
+                ring_down(step, sub).wait_send()
     for offset in range(n_z):
         across(offset).wait_send()
 
@@ -385,13 +468,13 @@
     steps = gate_table.shape[0]
     dma = pltpu.SemaphoreType.DMA
     dims = (n_tm, n_h, n_z, tokens, frame, features, shard)
-    weights = 3 + n_z + n_z
+    weights = 3 + 2 * n_z + n_z
     anywhere = pl.BlockSpec(memory_space=pl.ANY)
     out = jax.ShapeDtypeStruct((tokens, features), jnp.bfloat16)
     out_p, out_t = pl.pallas_call(
         functools.partial(kernel, dims),
         out_shape=(out, out),
-        in_specs=[pl.BlockSpec(memory_space=pltpu.SMEM)] + [anywhere] * 9,
+        in_specs=[pl.BlockSpec(memory_space=pltpu.HBM)] + [anywhere] * 9,
         out_specs=(pl.BlockSpec(memory_space=pltpu.VMEM),) * 2,
         scratch_shapes=[
             pltpu.VMEM((4, 2 * tokens + 4 * frame, features), jnp.bfloat16),
@@ -399,7 +482,9 @@
             pltpu.VMEM((2 * tokens, features), jnp.bfloat16),
             pltpu.VMEM((2, n_z, n_h * shard, features // 2), jnp.bfloat16),
             pltpu.VMEM((2, steps, features), jnp.float32),
-            dma((9,)),
+            pltpu.SMEM((1,), jnp.int32),
+            pltpu.SemaphoreType.REGULAR((2,)),
+            dma((10,)),
         ]
         + [dma((chunks,))] * 10
         + [dma((weights,))] * 2,

time: 85.5 us -> 70.7 us (0.83)
  the two profiles are of different devices: /device:TPU:112 before, /device:TPU:1 now
where the time goes in v2:
time: 70.7 us; the launch traced here: 70.5 us
  Pallas kernels  66.7 us (94%)
  local copies, waits for them, and re-layouts  2.57 us (4%)
  between operations  1.3 us (2%)
    pallas_call x1, Pallas kernels, local(): pl.pallas_call(functools.partial(kernel, dims), out_shape=(out, out), in_...  66.7 us
    unnamed x4, local copies, waits for them, and re-layouts  2.57 us

profile of v2, /device:TPU:1, one launch (start us, length us, event | category | flops | bytes accessed | tf_op | source)
XLA Modules:
  0.0 70.5 jit_solution(10104297875440683303)
XLA Ops:
  1.3 66.7 %tiled_attention.1 = (bf16[128,1536]{1,0:T(8,128)(2,1)}, bf16[128,1536]{1,0:T(8,128)(2,1)}) custom-call(s32[1]{0:T(128)S(6)} %copy.14.step_ref, bf16[128,1536]{1,0:T(8,128)(2,1)} %bitcast.11, bf16[128,1536]{1,0:T(8,128)(2,1)} %bitcast.12, bf16[128,1536]{1,0:T(8,128)(2,1)} %bitcast.13, bf16[128,1536]{1,0:T(8,128)(2,1)} %bitcast.14, ...), custom_call_target="tpu_custom_call" | custom-call | tf_op jit(solution)/shard_map/tiled_attention/pallas_call | solution.py:474
  68.0 0.0 copy-start
  68.0 1.8 %copy.15 = bf16[1,4,4,8,1536]{4,3,2,1,0:T(8,128)(2,1)} copy(bf16[1,4,4,8,1536]{4,3,2,1,0:T(8,128)(2,1)} %bitcast.10) | data formatting | bytes 786432
  69.8 0.0 copy-done
  69.8 0.7 %copy.16 = bf16[1,4,4,8,1536]{4,3,2,1,0:T(8,128)(2,1)} copy(bf16[1,4,4,8,1536]{4,3,2,1,0:T(8,128)(2,1)S(1)} %bitcast.9) | data formatting | bytes 786432
Async XLA Ops:
  68.0 1.8 %copy-start = (bf16[128,1536]{1,0:T(8,128)(2,1)S(1)}, bf16[128,1536]{1,0:T(8,128)(2,1)}, u32[]{:S(2)}) copy-start(bf16[128,1536]{1,0:T(8,128)(2,1)} %get-tuple-element.5) | copy-start | bytes 1179652

commit v3 on v2

--- a/solution.py
+++ b/solution.py
@@ -85,30 +85,29 @@
     even = lax.rem(tm + h + z, 2) == 0
     odd = jnp.logical_not(even)
     barrier = pltpu.get_barrier_semaphore()
-
-    def greet(semaphore):
-        for peer in (partner, gap):
-            pl.semaphore_signal(semaphore, inc=1, device_id=peer, device_id_type=MESH)
-
-        @pl.when(has_left)
-        def _():
-            pl.semaphore_signal(semaphore, inc=1, device_id=left, device_id_type=MESH)
-
-        @pl.when(has_right)
-        def _():
-            pl.semaphore_signal(semaphore, inc=1, device_id=right, device_id_type=MESH)
-
-    def greet_z(semaphore):
-        for peer in (above, below):
-            pl.semaphore_signal(semaphore, inc=1, device_id=peer, device_id_type=MESH)
+    always = tm >= 0
+    others = (
+        (gap, always, 1, 1),
+        (left, has_left, 3, 2),
+        (right, has_right, 2, 3),
+        (above, always, 5, 4),
+        (below, always, 4, 5),
+    )
+
+    def signal(semaphore, peer):
+        pl.semaphore_signal(semaphore, inc=1, device_id=peer, device_id_type=MESH)
 
     @pl.when(even)
     def _():
-        greet(barrier)
+        signal(barrier, partner)
 
     @pl.when(odd)
     def _():
-        greet_z(barrier)
+        for peer, exists, _, _ in others:
+
+            @pl.when(exists)
+            def _():
+                signal(barrier, peer)
 
     kv_loads = [
         pltpu.make_async_copy(ref, kv.at[i, pl.ds(own, tokens)], load_sem.at[i])
@@ -143,16 +142,14 @@
     def _():
         kv[:, pl.ds(right_own, rows), :] = jnp.zeros((4, rows, features), kv.dtype)
 
-    peers = 2 + has_left.astype(jnp.int32) + has_right.astype(jnp.int32)
-
     @pl.when(odd)
     def _():
-        pl.semaphore_wait(barrier, peers)
-        greet(hello.at[0])
+        pl.semaphore_wait(barrier, 1)
+        signal(hello.at[0], partner)
 
     @pl.when(even)
     def _():
-        pl.semaphore_wait(hello.at[0], peers)
+        pl.semaphore_wait(hello.at[0], 1)
 
     w_load.wait()
     for copy in kv_loads:
@@ -172,8 +169,19 @@
         cols = pl.ds(pl.multiple_of(g * wide, wide), wide)
         return kv.at[:, pl.ds(row, count), cols]
 
-    def to_partner(g):
-        return move(block(own, tokens, g), block(other, tokens, g), part_s.at[g], part_r.at[g], partner)
+    pieces = ((0, frame), (last, frame), (frame, tokens - 2 * frame))
+
+    def to_partner(g, piece):
+        row, count = pieces[piece]
+        slot = g * 3 + piece
+        return move(block(own + row, count, g), block(other + row, count, g), part_s.at[slot], part_r.at[slot], partner)
+
+    def send_edges(g):
+        to_partner(g, 0).start()
+        to_partner(g, 1).start()
+
+    def send_middle(g):
+        to_partner(g, 2).start()
 
     def own_left(g):
         return move(block(own, frame, g), block(right_own, frame, g), ownl_s.at[g], ownr_r.at[g], left)
@@ -224,18 +232,49 @@
         slot = 3 + 4 * hops + offset
         return move(ref, ref, ws.at[slot], wr.at[slot], sibling)
 
-    ahead = 3
+    crosses = jnp.logical_or(cross_left, cross_right)
     to_p.start()
+
+    def send_chunks(first, stop):
+        for k in range(first, stop):
+            if k == 0:
+                send_edges(0)
+            if k + 1 < chunks:
+                send_edges(k + 1)
+            send_middle(k)
+
+    send_chunks(0, 2)
+
+    @pl.when(jnp.logical_not(crosses))
+    def _():
+        send_chunks(2, chunks)
+
+    @pl.when(even)
+    def _():
+        count = 3 + has_left.astype(jnp.int32) + has_right.astype(jnp.int32)
+        pl.semaphore_wait(barrier, count)
+        for peer, exists, slot, _ in others:
+
+            @pl.when(exists)
+            def _():
+                signal(hello.at[slot], peer)
+
+    @pl.when(odd)
+    def _():
+        for _, exists, _, slot in others:
+
+            @pl.when(exists)
+            def _():
+                pl.semaphore_wait(hello.at[slot], 1)
+
     to_g.start()
-    for g in range(ahead):
-        to_partner(g).start()
 
     def send_own(g, carry):
-        @pl.when(has_left)
+        @pl.when(jnp.logical_and(has_left, jnp.logical_or(g < 2, jnp.logical_not(cross_left))))
         def _():
             own_left(g).start()
 
-        @pl.when(has_right)
+        @pl.when(jnp.logical_and(has_right, jnp.logical_or(g < 2, jnp.logical_not(cross_right))))
         def _():
             own_right(g).start()
 
@@ -245,16 +284,6 @@
 
     to_p.wait_recv()
     on_g.start()
-
-    @pl.when(even)
-    def _():
-        pl.semaphore_wait(barrier, 2)
-        greet_z(hello.at[1])
-
-    @pl.when(odd)
-    def _():
-        pl.semaphore_wait(hello.at[1], 2)
-
     ring_up(0, 0).start()
     ring_down(0, 0).start()
 
@@ -324,7 +353,18 @@
             ring_pass(g + 1, 0)
 
     def forward(g):
-        to_partner(g).wait_recv()
+        for k in range(2):
+
+            @pl.when(jnp.logical_and(cross_left, g < chunks // 2 - 1))
+            def _():
+                own_left(2 * g + 2 + k).start()
+
+            @pl.when(jnp.logical_and(cross_right, g < chunks // 2 - 1))
+            def _():
+                own_right(2 * g + 2 + k).start()
+
+        to_partner(g, 0).wait_recv()
+        to_partner(g, 1).wait_recv()
 
         @pl.when(jnp.logical_and(has_left, jnp.logical_not(cross_left)))
         def _():
@@ -334,33 +374,27 @@
         def _():
             relay_right(g).start()
 
-        early = chunks // 2
-
-        @pl.when(g < 2)
-        def _():
-            for k in range(early):
-                other_chunk = g * early + k
-
-                @pl.when(cross_left)
-                def _():
-                    own_right(other_chunk).wait_recv()
-                    cross_to_left(other_chunk).start()
-
-                @pl.when(cross_right)
-                def _():
-                    own_left(other_chunk).wait_recv()
-                    cross_to_right(other_chunk).start()
-
-        @pl.when(g == 0)
-        def _():
-            for k in range(ahead, chunks - 1):
-                to_partner(k).start()
-
-        @pl.when(g == 1)
-        def _():
-            to_partner(chunks - 1).start()
+        @pl.when(cross_left)
+        def _():
+            own_right(g).wait_recv()
+            cross_to_left(g).start()
+
+        @pl.when(cross_right)
+        def _():
+            own_left(g).wait_recv()
+            cross_to_right(g).start()
+
+        @pl.when(jnp.logical_and(crosses, g < chunks - 2))
+        def _():
+            @pl.when(g < chunks - 3)
+            def _():
+                send_edges(g + 3)
+
+            send_middle(g + 2)
 
     def compute(g):
+        to_partner(g, 2).wait_recv()
+
         @pl.when(jnp.logical_and(has_left, jnp.logical_not(cross_left)))
         def _():
             own_right(g).wait_recv()
@@ -380,6 +414,9 @@
         for head in range(PAIR):
             attend(pl.ds(pl.multiple_of(g * wide + head * HD, HD), HD))
 
+    lag = jnp.where(crosses, 2, 1)
+    shift = jnp.where(z < 2, 2, jnp.where(z < n_z // 2, 1, 0))
+
     def chunk(g, carry):
         @pl.when(g < chunks)
         def _():
@@ -387,17 +424,17 @@
 
         for stage in range(hops + 1):
 
-            @pl.when(g == stage)
+            @pl.when(g == stage + shift)
             def _():
                 ring_stage(stage)
 
-        @pl.when(g >= 1)
-        def _():
-            compute(g - 1)
+        @pl.when(jnp.logical_and(g >= lag, g < chunks + lag))
+        def _():
+            compute(g - lag)
 
         return carry
 
-    lax.fori_loop(0, chunks + 1, chunk, 0)
+    lax.fori_loop(0, chunks + 2, chunk, 0)
 
     step_load.wait()
     for copy in gate_loads:
@@ -429,7 +466,8 @@
         outt_ref[:, outs] = tangent.astype(outt_ref.dtype)
 
     def finish(g, carry):
-        to_partner(g).wait_send()
+        for piece in range(3):
+            to_partner(g, piece).wait_send()
 
         @pl.when(has_left)
         def _():
@@ -464,7 +502,7 @@
     shard = weight.shape[1]
     n_tm, n_h, n_z = sizes
     chunks = features // (PAIR * HD)
-    flat = [a.reshape(tokens, features) for a in (q, k, v, qt, kt, vt)]
+    flat = [pltpu.with_memory_space_constraint(a.reshape(tokens, features), pltpu.HBM) for a in (q, k, v, qt, kt, vt)]
     steps = gate_table.shape[0]
     dma = pltpu.SemaphoreType.DMA
     dims = (n_tm, n_h, n_z, tokens, frame, features, shard)
@@ -483,14 +521,15 @@
             pltpu.VMEM((2, n_z, n_h * shard, features // 2), jnp.bfloat16),
             pltpu.VMEM((2, steps, features), jnp.float32),
             pltpu.SMEM((1,), jnp.int32),
-            pltpu.SemaphoreType.REGULAR((2,)),
+            pltpu.SemaphoreType.REGULAR((6,)),
             dma((10,)),
         ]
-        + [dma((chunks,))] * 10
+        + [dma((3 * chunks,))] * 2
+        + [dma((chunks,))] * 8
         + [dma((weights,))] * 2,
-        compiler_params=pltpu.CompilerParams(collective_id=0, has_side_effects=True),
+        compiler_params=pltpu.CompilerParams(vmem_limit_bytes=24 << 20, collective_id=0, has_side_effects=True),
         name="tiled_attention",
-    )(timestep, *flat, weight.T, gate_table, gate_slope)
+    )(timestep, *flat, *(pltpu.with_memory_space_constraint(a, pltpu.HBM) for a in (weight.T, gate_table, gate_slope)))
     return (out_p.reshape(q.shape), out_t.reshape(q.shape))
 
 

time: 70.7 us -> 64.4 us (0.911)
  Pallas kernels: 66.7 us -> 61.5 us
  local copies, waits for them, and re-layouts: 2.57 us -> 1.49 us
    pallas_call x1, Pallas kernels: 66.7 us -> 61.5 us  [local(): pl.pallas_call(functools.partial(kernel, dims), out_shape=(out, out), in_...]
    unnamed x4 -> x2, local copies, waits for them, and re-layouts: 2.57 us -> 1.49 us
where the time goes in v3:
time: 64.4 us; the launch traced here: 64.3 us
  Pallas kernels  61.5 us (95%)
  local copies, waits for them, and re-layouts  1.49 us (2%)
  between operations  1.29 us (2%)
    pallas_call x1, Pallas kernels, local(): pl.pallas_call(functools.partial(kernel, dims), out_shape=(out, out), in_...  61.5 us
    unnamed x2, local copies, waits for them, and re-layouts  1.49 us

profile of v3, /device:TPU:1, one launch (start us, length us, event | category | flops | bytes accessed | tf_op | source)
XLA Modules:
  0.0 64.3 jit_solution(7872822941284845756)
XLA Ops:
  1.3 61.5 %tiled_attention.1 = (bf16[128,1536]{1,0:T(8,128)(2,1)S(1)}, bf16[128,1536]{1,0:T(8,128)(2,1)S(1)}) custom-call(s32[1]{0:T(128)S(6)} %copy.14.step_ref, bf16[128,1536]{1,0:T(8,128)(2,1)} %bitcast.11, bf16[128,1536]{1,0:T(8,128)(2,1)} %bitcast.12, bf16[128,1536]{1,0:T(8,128)(2,1)} %bitcast.13, bf16[128,1536]{1,0:T(8,128)(2,1)} %bitcast.14, ...), custom_call_target="tpu_custom_call" | custom-call | tf_op jit(solution)/shard_map/tiled_attention/pallas_call | solution.py:512
  62.8 0.7 %copy.15 = bf16[1,4,4,8,1536]{4,3,2,1,0:T(8,128)(2,1)} copy(bf16[1,4,4,8,1536]{4,3,2,1,0:T(8,128)(2,1)S(1)} %bitcast.10) | data formatting | bytes 786432
  63.5 0.7 %copy.16 = bf16[1,4,4,8,1536]{4,3,2,1,0:T(8,128)(2,1)} copy(bf16[1,4,4,8,1536]{4,3,2,1,0:T(8,128)(2,1)S(1)} %bitcast.9) | data formatting | bytes 786432

commit v4 on v3

--- a/solution.py
+++ b/solution.py
@@ -270,11 +270,11 @@
     to_g.start()
 
     def send_own(g, carry):
-        @pl.when(jnp.logical_and(has_left, jnp.logical_or(g < 2, jnp.logical_not(cross_left))))
+        @pl.when(jnp.logical_and(has_left, jnp.logical_not(cross_left)))
         def _():
             own_left(g).start()
 
-        @pl.when(jnp.logical_and(has_right, jnp.logical_or(g < 2, jnp.logical_not(cross_right))))
+        @pl.when(jnp.logical_and(has_right, jnp.logical_not(cross_right)))
         def _():
             own_right(g).start()
 
@@ -353,15 +353,21 @@
             ring_pass(g + 1, 0)
 
     def forward(g):
-        for k in range(2):
-
-            @pl.when(jnp.logical_and(cross_left, g < chunks // 2 - 1))
-            def _():
-                own_left(2 * g + 2 + k).start()
-
-            @pl.when(jnp.logical_and(cross_right, g < chunks // 2 - 1))
-            def _():
-                own_right(2 * g + 2 + k).start()
+        @pl.when(jnp.logical_and(cross_left, g == 0))
+        def _():
+            own_left(0).start()
+
+        @pl.when(jnp.logical_and(cross_right, g == 0))
+        def _():
+            own_right(0).start()
+
+        @pl.when(jnp.logical_and(cross_left, g < chunks - 1))
+        def _():
+            own_left(g + 1).start()
+
+        @pl.when(jnp.logical_and(cross_right, g < chunks - 1))
+        def _():
+            own_right(g + 1).start()
 
         to_partner(g, 0).wait_recv()
         to_partner(g, 1).wait_recv()

time: 64.4 us -> 62 us (0.963)
  Pallas kernels: 61.5 us -> 59.1 us
    pallas_call x1, Pallas kernels: 61.5 us -> 59.1 us  [local(): pl.pallas_call(functools.partial(kernel, dims), out_shape=(out, out), in_...]
where the time goes in v4:
time: 62 us; the launch traced here: 61.8 us
  Pallas kernels  59.1 us (95%)
  local copies, waits for them, and re-layouts  1.49 us (2%)
  between operations  1.29 us (2%)
    pallas_call x1, Pallas kernels, local(): pl.pallas_call(functools.partial(kernel, dims), out_shape=(out, out), in_...  59.1 us
    unnamed x2, local copies, waits for them, and re-layouts  1.49 us

profile of v4, /device:TPU:1, one launch (start us, length us, event | category | flops | bytes accessed | tf_op | source)
XLA Modules:
  0.0 61.8 jit_solution(8280057080599739769)
XLA Ops:
  1.3 59.1 %tiled_attention.1 = (bf16[128,1536]{1,0:T(8,128)(2,1)S(1)}, bf16[128,1536]{1,0:T(8,128)(2,1)S(1)}) custom-call(s32[1]{0:T(128)S(6)} %copy.14.step_ref, bf16[128,1536]{1,0:T(8,128)(2,1)} %bitcast.11, bf16[128,1536]{1,0:T(8,128)(2,1)} %bitcast.12, bf16[128,1536]{1,0:T(8,128)(2,1)} %bitcast.13, bf16[128,1536]{1,0:T(8,128)(2,1)} %bitcast.14, ...), custom_call_target="tpu_custom_call" | custom-call | tf_op jit(solution)/shard_map/tiled_attention/pallas_call | solution.py:518
  60.3 0.7 %copy.15 = bf16[1,4,4,8,1536]{4,3,2,1,0:T(8,128)(2,1)} copy(bf16[1,4,4,8,1536]{4,3,2,1,0:T(8,128)(2,1)S(1)} %bitcast.10) | data formatting | bytes 786432
  61.1 0.7 %copy.16 = bf16[1,4,4,8,1536]{4,3,2,1,0:T(8,128)(2,1)} copy(bf16[1,4,4,8,1536]{4,3,2,1,0:T(8,128)(2,1)S(1)} %bitcast.9) | data formatting | bytes 786432

commit v5 on v4

--- a/solution.py
+++ b/solution.py
@@ -422,6 +422,7 @@
 
     lag = jnp.where(crosses, 2, 1)
     shift = jnp.where(z < 2, 2, jnp.where(z < n_z // 2, 1, 0))
+    shift = jnp.where(tm + h + z == 0, 0, shift)
 
     def chunk(g, carry):
         @pl.when(g < chunks)

time: 62 us -> 61.4 us (level)
  Pallas kernels: 59.1 us -> 58.4 us
    pallas_call x1, Pallas kernels: 59.1 us -> 58.4 us  [local(): pl.pallas_call(functools.partial(kernel, dims), out_shape=(out, out), in_...]
where the time goes in v5:
time: 61.4 us; the launch traced here: 61.2 us
  Pallas kernels  58.4 us (95%)
  local copies, waits for them, and re-layouts  1.49 us (2%)
  between operations  1.29 us (2%)
    pallas_call x1, Pallas kernels, local(): pl.pallas_call(functools.partial(kernel, dims), out_shape=(out, out), in_...  58.4 us
    unnamed x2, local copies, waits for them, and re-layouts  1.49 us

profile of v5, /device:TPU:1, one launch (start us, length us, event | category | flops | bytes accessed | tf_op | source)
XLA Modules:
  0.0 61.2 jit_solution(2317984883021741255)
XLA Ops:
  1.3 58.4 %tiled_attention.1 = (bf16[128,1536]{1,0:T(8,128)(2,1)S(1)}, bf16[128,1536]{1,0:T(8,128)(2,1)S(1)}) custom-call(s32[1]{0:T(128)S(6)} %copy.14.step_ref, bf16[128,1536]{1,0:T(8,128)(2,1)} %bitcast.11, bf16[128,1536]{1,0:T(8,128)(2,1)} %bitcast.12, bf16[128,1536]{1,0:T(8,128)(2,1)} %bitcast.13, bf16[128,1536]{1,0:T(8,128)(2,1)} %bitcast.14, ...), custom_call_target="tpu_custom_call" | custom-call | tf_op jit(solution)/shard_map/tiled_attention/pallas_call | solution.py:519
  59.7 0.7 %copy.15 = bf16[1,4,4,8,1536]{4,3,2,1,0:T(8,128)(2,1)} copy(bf16[1,4,4,8,1536]{4,3,2,1,0:T(8,128)(2,1)S(1)} %bitcast.10) | data formatting | bytes 786432
  60.5 0.7 %copy.16 = bf16[1,4,4,8,1536]{4,3,2,1,0:T(8,128)(2,1)} copy(bf16[1,4,4,8,1536]{4,3,2,1,0:T(8,128)(2,1)S(1)} %bitcast.9) | data formatting | bytes 786432
